TPU v7x, 512 devices: a whole 4x4x16 slice. The times are simulated.
512 devices in a mesh: seq: 16 (over y, x), mp: 32 (over z, core).
Axes of the slice: x: 4, y: 4, z: 16, core: 2. Of those that a mesh axis runs over, the one named last changes fastest.
Arguments:
- q_proj: bfloat16 [4096, 8192], P('seq', 'mp'), may hold values from -6 to 6
- k_proj: bfloat16 [4096, 8192], P('seq', 'mp'), may hold values from -6 to 6
- v_proj: bfloat16 [4096, 8192], P('seq', 'mp'), may hold values from -6 to 6
- out_grad: bfloat16 [4096, 8192], P('seq', 'mp'), may hold values from -0.75 to 0.75
- out_weight: bfloat16 [8192, 8192], P('mp', 'seq'), may hold values from -0.0625 to 0.0625
- taps: float32 [7, 512], P(None, 'mp'), may hold values from -2.4 to 2.4
Outputs:
- grad_q: bfloat16 [4096, 8192], P('seq', 'mp')
- grad_k: bfloat16 [4096, 8192], P('seq', 'mp')
- grad_v: bfloat16 [4096, 8192], P('seq', 'mp')
- grad_weight: float32 [8192, 8192], P('mp', 'seq')
- grad_taps: float32 [7, 512], P(None, 'mp')
All inputs are finite; a program needn't handle non-finite values.
Results may differ from a plain program's by a relative error of at most 0.0029.
Values may be sent and summed in bfloat16 or wider, within the bound.
A program may use at most 64 MiB of HBM per device.

v0:
```python
import jax
import jax.numpy as jnp
from jax import lax
from jax.sharding import PartitionSpec as P

TAPS = 7
GROUP = 16


def passed_along(array, axis, by):
    count = lax.axis_size(axis)
    pairs = [(i, i + by) for i in range(count) if 0 <= i + by < count]
    return lax.ppermute(array, axis, pairs)


def shards(q_proj, k_proj, v_proj, out_grad, out_weight, taps):
    tokens, channels = q_proj.shape
    rim_rows = TAPS - 1
    q_full = q_proj.astype(jnp.float32)
    k_full = k_proj.astype(jnp.float32)
    v_full = v_proj.astype(jnp.float32)
    spread = jnp.broadcast_to(taps[:, :, None], (TAPS, taps.shape[1], GROUP)).reshape(
        TAPS, channels
    )
    tail_rows = jnp.stack([k_proj[tokens - rim_rows :], v_proj[tokens - rim_rows :]])
    before = passed_along(tail_rows, "seq", 1)
    keys_wide = jnp.concatenate([before[0], k_proj], 0).astype(jnp.float32)
    values_wide = jnp.concatenate([before[1], v_proj], 0).astype(jnp.float32)
    product = keys_wide * values_wide
    filtered = jnp.zeros((tokens, channels), jnp.float32)
    for offset in range(TAPS):
        filtered = (
            filtered + spread[offset] * product[rim_rows - offset : rim_rows - offset + tokens]
        )
    gated = (q_full * filtered).astype(jnp.bfloat16)
    seq_count, mp_count = (lax.axis_size("seq"), lax.axis_size("mp"))
    cores = mp_count // seq_count
    pairs = [
        (t * mp_count + cores * z + c, z * mp_count + cores * t + c)
        for t in range(seq_count)
        for z in range(seq_count)
        for c in range(cores)
    ]
    crossed = lax.ppermute(out_grad, ("seq", "mp"), pairs)
    tiles = lax.all_gather(crossed, "mp", axis=0)
    columns = (
        tiles.reshape(seq_count, cores, tokens, channels)
        .transpose(0, 2, 1, 3)
        .reshape(seq_count * tokens, cores * channels)
    )
    partial = lax.dot_general(
        columns, out_weight, (((1,), (1,)), ((), ())), preferred_element_type=jnp.float32
    )
    grad_gated = lax.psum_scatter(partial, "seq", scatter_dimension=0, tiled=True)
    grad_weight = lax.dot_general(
        lax.all_gather(gated, "seq", axis=0, tiled=True),
        columns,
        (((0,), (0,)), ((), ())),
        preferred_element_type=jnp.float32,
    )
    grad_q = (grad_gated * filtered).astype(jnp.bfloat16)
    grad_filtered = grad_gated * q_full
    following = passed_along(grad_filtered[:rim_rows], "seq", -1)
    grad_ext = jnp.concatenate([grad_filtered, following], 0)
    grad_product = jnp.zeros((tokens, channels), jnp.float32)
    for offset in range(TAPS):
        grad_product = grad_product + spread[offset] * grad_ext[offset : offset + tokens]
    grad_k = (grad_product * v_full).astype(jnp.bfloat16)
    grad_v = (grad_product * k_full).astype(jnp.bfloat16)
    filter_terms = jnp.stack(
        [
            jnp.sum(grad_filtered * product[rim_rows - offset : rim_rows - offset + tokens], 0)
            for offset in range(TAPS)
        ]
    )
    filter_local = filter_terms.reshape(TAPS, channels // GROUP, GROUP).sum(-1)
    grad_taps = lax.psum(filter_local, "seq")
    return (grad_q, grad_k, grad_v, grad_weight, grad_taps)


def solution(mesh):
    placed = (
        P("seq", "mp"),
        P("seq", "mp"),
        P("seq", "mp"),
        P("seq", "mp"),
        P("mp", "seq"),
        P(None, "mp"),
    )
    return jax.shard_map(
        shards,
        mesh=mesh,
        in_specs=placed,
        out_specs=(P("seq", "mp"), P("seq", "mp"), P("seq", "mp"), P("mp", "seq"), P(None, "mp")),
        check_vma=False,
    )
```

profile of v0, /device:TPU:32, one launch (start us, length us, event | category | flops | bytes accessed | tf_op | source)
XLA Modules:
  0.0 327.7 jit_solution(6569584320959466278)
XLA Ops:
  7.2 0.0 copy-start
  7.2 0.0 all-gather.6.cloned.1.call-start
  7.2 3.1 collective-permute-start
  10.3 12.5 %collective-permute-done = bf16[256,256]{1,0:T(8,128)(2,1)S(1)} collective-permute-done((bf16[256,256]{1,0:T(8,128)(2,1)}, bf16[256,256]{1,0:T(8,128)(2,1)S(1)}, u32[]{:S(2)}, u32[]{:S(2)}) %collective-permute-start) | collective-permute-done | bytes 131104 | tf_op jit(solution)/shard_map/ppermute | solution.py:44
  22.8 0.0 copy-start.5
  22.8 0.7 copy-done.5
  23.5 0.0 all-gather.6.cloned.1.call-update
  23.5 0.0 all-gather.4.cloned.1.call-start
  23.5 0.7 slice_bitcast_fusion.2
  24.3 1.3 collective-permute-start.1
  25.6 0.9 slice_bitcast_fusion.10
  26.5 0.1 broadcast_in_dim.44
  26.6 0.1 broadcast_in_dim.45
  26.7 0.1 broadcast_in_dim.42
  26.8 0.1 broadcast_in_dim.43
  26.8 0.1 broadcast_in_dim.40
  26.9 0.1 broadcast_in_dim.41
  27.0 0.1 broadcast_in_dim.38
  27.1 0.1 broadcast_in_dim.39
  27.1 0.1 broadcast_in_dim.36
  27.2 0.1 broadcast_in_dim.37
  27.3 0.1 broadcast_in_dim.34
  27.4 0.1 broadcast_in_dim.35
  27.4 0.1 broadcast_in_dim.32
  27.5 0.1 broadcast_in_dim.33
  27.6 0.0 collective-permute-done.1
  27.6 1.0 convert_multiply_fusion.2
  28.7 1.8 fusion
  30.5 0.0 all-gather.4.cloned.1.call-update
  30.5 0.0 reduce-scatter.2.cloned.1.call-start
  30.6 87.3 %all-gather.6.cloned.1.call-done = bf16[8192,256]{1,0:T(8,128)(2,1)} async-done(((bf16[256,256]{1,0:T(8,128)(2,1)}), bf16[8192,256]{1,0:T(8,128)(2,1)}) %all-gather.6.cloned.1.call-update) | async-done | bytes 4194320 | tf_op jit(solution)/shard_map/all_gather | solution.py:45
  117.8 8.0 %copy.12 = bf16[16,2,256,256]{2,0,3,1:T(8,128)(2,1)} copy(bf16[16,2,256,256]{3,2,1,0:T(8,128)(2,1)} %bitcast.36) | data formatting | bytes 8388608 | tf_op jit(solution)/shard_map/reshape | solution.py:47
  125.8 4.4 %copy.13 = bf16[64,8,16,256]{3,1,2,0:T(8,128)(2,1)S(1)} copy(bf16[64,8,16,256]{3,2,1,0:T(8,128)(2,1)} %bitcast.35) | data formatting | bytes 8388608
  130.2 0.0 copy-start.1
  130.2 2.0 copy-done.1
  132.2 0.0 copy-done
  132.2 3.2 fusion.19
  135.4 0.0 reduce-scatter.2.cloned.1.call-update
  135.4 0.0 copy-start.4
  135.4 0.0 copy-start.2
  135.4 0.0 copy-start.3
  135.5 43.0 %all-gather.4.cloned.1.call-done = bf16[4096,256]{1,0:T(8,128)(2,1)} async-done(((bf16[256,256]{1,0:T(8,128)(2,1)}), bf16[4096,256]{1,0:T(8,128)(2,1)}) %all-gather.4.cloned.1.call-update) | async-done | bytes 2097168 | tf_op jit(solution)/shard_map/all_gather | solution.py:56
  178.5 4.9 %fusion.20 = f32[256,512]{1,0:T(8,128)} fusion(bf16[4096,256]{1,0:T(8,128)(2,1)} %all-gather.4.cloned.1.call-done, bf16[4096,512]{0,1:T(8,128)(2,1)} %bitcast.34), kind=kOutput, calls=%fused_computation.61 | convolution fusion | flops 1073741824 | bytes 6815744 | tf_op jit(solution)/shard_map/dot_general | solution.py:55
  183.4 91.8 %reduce-scatter.2.cloned.1.call-done = f32[256,256]{1,0:T(8,128)} async-done(((f32[4096,256]{1,0:T(8,128)}), f32[256,256]{1,0:T(8,128)}) %reduce-scatter.2.cloned.1.call-update) | async-done | bytes 262160 | tf_op jit(solution)/shard_map/reduce_scatter | solution.py:54
  275.2 0.0 copy-done.4
  275.2 1.9 multiply_reduce_fusion
  277.1 1.3 collective-permute-start.2
  278.4 0.1 stack.36
  278.4 0.1 stack.37
  278.5 0.1 stack.38
  278.6 0.1 stack.39
  278.7 0.1 stack.40
  278.8 0.1 stack.41
  278.8 0.1 stack.42
  279.0 0.1 reduce_sum.79
  279.1 40.5 %psum.7 = f32[7,16]{1,0:T(8,128)} all-reduce(f32[7,16]{1,0:T(8,128)S(1)} %reduce_sum.79), channel_id=1, replica_groups=mesh['seq'=16,'mp'=32] {'seq'}, use_global_device_ids=true, to_apply=%region_9.0 | all-reduce | flops 112 | bytes 896 | tf_op jit(solution)/shard_map/psum | solution.py:77
  319.6 0.0 collective-permute-done.2
  319.6 0.0 copy-done.2
  319.6 0.9 multiply_convert_fusion
  320.5 0.0 copy-done.3
  320.5 0.7 multiply_convert_fusion.1
  (10 shorter events, 0.1 us)
Async XLA Ops:
  7.2 125.0 %copy-start = (bf16[256,512]{1,0:T(8,128)(2,1)S(1)}, bf16[256,512]{1,0:T(8,128)(2,1)}, u32[]{:S(2)}) copy-start(bf16[256,512]{1,0:T(8,128)(2,1)} %param.10) | copy-start | bytes 786436
  7.2 110.7 %all-gather.6.cloned.1.call-start = ((), (), s32[]{:S(2)}) async-start(), calls=%async_computation.3 | async-start | bytes 4325376 | tf_op jit(solution)/shard_map/all_gather | solution.py:45
  7.2 15.6 %collective-permute-start = (bf16[256,256]{1,0:T(8,128)(2,1)}, bf16[256,256]{1,0:T(8,128)(2,1)S(1)}, u32[]{:S(2)}, u32[]{:S(2)}) collective-permute-start(bf16[256,256]{1,0:T(8,128)(2,1)} %param.9), channel_id=1, source_target_pairs={{0,0},{1,1},{2,32},{3,33},{4,64},{5,65},{6,96},{7,97},{8,128},{9,1... | collective-permute-start | bytes 393224 | tf_op jit(solution)/shard_map/ppermute | solution.py:44
  22.8 0.7 copy-start.5
  23.5 155.0 %all-gather.4.cloned.1.call-start = ((), (), s32[]{:S(2)}) async-start(), calls=%async_computation.2 | async-start | bytes 2228224 | tf_op jit(solution)/shard_map/all_gather | solution.py:56
  24.3 3.3 %collective-permute-start.1 = (bf16[2,6,256]{2,1,0:T(8,128)(2,1)S(1)}, bf16[2,6,256]{2,1,0:T(8,128)(2,1)S(1)}, u32[]{:S(2)}, u32[]{:S(2)}) collective-permute-start(bf16[2,6,256]{2,1,0:T(8,128)(2,1)S(1)} %pad_maximum_fusion.1), channel_id=1, source_target_pairs={{0,32},{32,64},{64,96},{96,128},{128,160},{160,192},{192,224},{224... | collective-permute-start | bytes 18440 | tf_op jit(solution)/shard_map/ppermute | solution.py:13
  30.5 244.7 %reduce-scatter.2.cloned.1.call-start = ((), (), s32[]{:S(2)}) async-start(), calls=%async_computation.1 | async-start | bytes 4456448 | tf_op jit(solution)/shard_map/reduce_scatter | solution.py:54
  130.2 2.0 copy-start.1
  135.4 139.8 %copy-start.4 = (bf16[256,256]{1,0:T(8,128)(2,1)S(1)}, bf16[256,256]{1,0:T(8,128)(2,1)}, u32[]{:S(2)}) copy-start(bf16[256,256]{1,0:T(8,128)(2,1)} %param.6) | copy-start | bytes 393220
  135.4 184.1 %copy-start.2 = (bf16[256,256]{1,0:T(8,128)(2,1)S(1)}, bf16[256,256]{1,0:T(8,128)(2,1)}, u32[]{:S(2)}) copy-start(bf16[256,256]{1,0:T(8,128)(2,1)} %param.7) | copy-start | bytes 393220
  135.4 185.0 %copy-start.3 = (bf16[256,256]{1,0:T(8,128)(2,1)S(1)}, bf16[256,256]{1,0:T(8,128)(2,1)}, u32[]{:S(2)}) copy-start(bf16[256,256]{1,0:T(8,128)(2,1)} %param.8) | copy-start | bytes 393220
  277.1 42.5 %collective-permute-start.2 = (f32[6,256]{1,0:T(8,128)S(1)}, f32[6,256]{1,0:T(8,128)S(1)}, u32[]{:S(2)}, u32[]{:S(2)}) collective-permute-start(f32[6,256]{1,0:T(8,128)S(1)} %slice.158), channel_id=1, source_target_pairs={{32,0},{64,32},{96,64},{128,96},{160,128},{192,160},{224,192},{256... | collective-permute-start | bytes 18440 | tf_op jit(solution)/shard_map/ppermute | solution.py:13
Sparse Core Ops, SparseCore 0:
  23.6 94.1 all-gather.5
  121.4 57.0 all-gather.3
  182.7 92.4 reduce-scatter.1
where the time goes:
time: 328 us
  waiting for transfers between devices  235 us (72%)
  blocking collectives  40.5 us (12%)
  local copies, waits for them, and re-layouts  18.3 us (6%)
  between operations  13.9 us (4%)
  matrix products  8.15 us (2%)
  other arithmetic  6.39 us (2%)
  starting transfers between devices  5.76 us (2%)
    reduce_scatter x1, waiting for transfers between devices, shards(): lax.psum_scatter(partial, 'seq', scatter_dimension=0, tiled=True)  91.8 us
    all_gather x1, waiting for transfers between devices, shards(): tiles = lax.all_gather(crossed, 'mp', axis=0)  87.3 us
    all_gather x1, waiting for transfers between devices, shards(): lax.all_gather(gated, 'seq', axis=0, tiled=True)  43 us
    psum x1, blocking collectives, shards(): grad_taps = lax.psum(filter_local, 'seq')  40.5 us
    ppermute x1, waiting for transfers between devices, shards(): crossed = lax.ppermute(out_grad, ('seq', 'mp'), pairs)  12.5 us
    reshape x1, local copies, waits for them, and re-layouts, shards(): tiles.reshape(seq_count, cores, tokens, channels).transpose(0, 2, 1, 3)  7.96 us
    unnamed x19, local copies, waits for them, and re-layouts  7.08 us
  transfers between devices with their start and end apart: 6, of which 4 were waited for; matrix products, arithmetic and copies ran while one was open for 8% of the time, Pallas kernels for 0%

commit v1 on v0

--- a/solution.py
+++ b/solution.py
@@ -74,7 +74,11 @@
         ]
     )
     filter_local = filter_terms.reshape(TAPS, channels // GROUP, GROUP).sum(-1)
-    grad_taps = lax.psum(filter_local, "seq")
+    grad_taps = filter_local
+    for hop in (1, 2, 4, 8):
+        grad_taps = grad_taps + lax.ppermute(
+            grad_taps, "seq", [(dev, dev ^ hop) for dev in range(16)]
+        )
     return (grad_q, grad_k, grad_v, grad_weight, grad_taps)
 
 

time: 328 us -> 304 us (0.927)
  the two profiles are of different devices: /device:TPU:32 before, /device:TPU:1 now
where the time goes in v1:
time: 304 us; the launch traced here: 303 us
  waiting for transfers between devices  236 us (78%)
  starting transfers between devices  22.5 us (7%)
  local copies, waits for them, and re-layouts  17.5 us (6%)
  between operations  13.9 us (5%)
  matrix products  8.19 us (3%)
  other arithmetic  5.12 us (2%)
    all_gather x1, waiting for transfers between devices, shards(): tiles = lax.all_gather(crossed, 'mp', axis=0)  110 us
    reduce_scatter x1, waiting for transfers between devices, shards(): lax.psum_scatter(partial, 'seq', scatter_dimension=0, tiled=True)  81.6 us
    all_gather x1, waiting for transfers between devices, shards(): lax.all_gather(gated, 'seq', axis=0, tiled=True)  41.1 us
    ppermute x4, starting transfers between devices, shards(): lax.ppermute(grad_taps, 'seq', [(dev, dev ^ hop) for dev in range(16)])  16 us
    unnamed x21, local copies, waits for them, and re-layouts  7.91 us
    reshape x1, local copies, waits for them, and re-layouts, shards(): tiles.reshape(seq_count, cores, tokens, channels).transpose(0, 2, 1, 3)  7.91 us
  transfers between devices with their start and end apart: 10, of which 6 were waited for; matrix products, arithmetic and copies ran while one was open for 3% of the time, Pallas kernels for 0%

profile of v1, /device:TPU:1, one launch (start us, length us, event | category | flops | bytes accessed | tf_op | source)
XLA Modules:
  0.0 303.1 jit_solution(15161105057952484674)
XLA Ops:
  7.2 0.0 copy-start
  7.2 0.0 all-gather.6.cloned.1.call-start
  7.2 1.7 collective-permute-start
  8.9 0.0 collective-permute-done
  8.9 0.7 copy-done.5
  9.6 0.0 all-gather.6.cloned.1.call-update
  9.6 0.0 reduce-scatter.2.cloned.1.call-start
  9.7 109.5 %all-gather.6.cloned.1.call-done = bf16[8192,256]{1,0:T(8,128)(2,1)} async-done(((bf16[256,256]{1,0:T(8,128)(2,1)}), bf16[8192,256]{1,0:T(8,128)(2,1)}) %all-gather.6.cloned.1.call-update) | async-done | bytes 4194320 | tf_op jit(solution)/shard_map/all_gather | solution.py:45
  119.2 7.9 %copy.12 = bf16[16,2,256,256]{2,0,3,1:T(8,128)(2,1)} copy(bf16[16,2,256,256]{3,2,1,0:T(8,128)(2,1)} %bitcast.36) | data formatting | bytes 8388608 | tf_op jit(solution)/shard_map/reshape | solution.py:47
  127.1 4.4 %copy.13 = bf16[64,8,16,256]{3,1,2,0:T(8,128)(2,1)S(1)} copy(bf16[64,8,16,256]{3,2,1,0:T(8,128)(2,1)} %bitcast.35) | data formatting | bytes 8388608
  131.5 0.0 copy-start.1
  131.5 1.9 copy-done.1
  133.4 0.0 copy-done
  133.4 3.3 %fusion.19 = f32[4096,256]{1,0:T(8,128)} fusion(bf16[4096,512]{0,1:T(8,128)(2,1)S(1)} %bitcast.33, bf16[256,512]{1,0:T(8,128)(2,1)S(1)} %copy-done), kind=kOutput, calls=%fused_computation.60 | convolution fusion | flops 1073741824 | bytes 8650752 | tf_op jit(solution)/shard_map/dot_general | solution.py:51
  136.7 0.0 reduce-scatter.2.cloned.1.call-update
  136.7 0.0 all-gather.4.cloned.1.call-start
  136.8 0.8 copy-done.2
  137.6 0.1 copy-done.3
  137.7 3.4 %collective-permute-start.1 = (bf16[2,6,256]{2,1,0:T(8,128)(2,1)S(1)}, bf16[2,6,256]{2,1,0:T(8,128)(2,1)S(1)}, u32[]{:S(2)}, u32[]{:S(2)}) collective-permute-start(bf16[2,6,256]{2,1,0:T(8,128)(2,1)S(1)} %pad_maximum_fusion.1), channel_id=1, source_target_pairs={{0,32},{32,64},{64,96},{96,128},{128,160},{160,192},{192,224},{224... | collective-permute-start | bytes 18440 | tf_op jit(solution)/shard_map/ppermute | solution.py:13
  141.1 0.0 copy-done.6
  141.1 0.1 broadcast_in_dim.44
  141.2 0.1 broadcast_in_dim.45
  141.3 0.1 broadcast_in_dim.42
  141.3 0.1 broadcast_in_dim.43
  141.4 0.1 broadcast_in_dim.40
  141.5 0.1 broadcast_in_dim.41
  141.6 0.1 broadcast_in_dim.38
  141.7 0.1 broadcast_in_dim.39
  141.7 0.1 broadcast_in_dim.36
  141.8 0.1 broadcast_in_dim.37
  141.9 0.1 broadcast_in_dim.34
  142.0 0.1 broadcast_in_dim.35
  142.0 0.1 broadcast_in_dim.32
  142.1 0.1 broadcast_in_dim.33
  142.2 0.0 collective-permute-done.1
  142.2 0.1 convert_multiply_fusion.2
  142.3 0.0 copy-done.4
  142.3 0.9 fusion
  143.2 0.0 all-gather.4.cloned.1.call-update
  143.2 81.6 %reduce-scatter.2.cloned.1.call-done = f32[256,256]{1,0:T(8,128)} async-done(((f32[4096,256]{1,0:T(8,128)}), f32[256,256]{1,0:T(8,128)}) %reduce-scatter.2.cloned.1.call-update) | async-done | bytes 262160 | tf_op jit(solution)/shard_map/reduce_scatter | solution.py:54
  224.9 1.9 multiply_reduce_fusion
  226.8 0.1 stack.36
  226.8 0.1 stack.37
  226.9 0.1 stack.38
  227.0 0.1 stack.39
  227.1 0.1 stack.40
  227.1 0.1 stack.41
  227.2 0.1 stack.42
  227.4 0.1 reduce_sum.79
  227.5 2.9 collective-permute-start.3
  230.4 1.5 collective-permute-done.3
  231.8 4.0 %collective-permute-start.4 = (f32[7,16]{1,0:T(8,128)S(1)}, f32[7,16]{1,0:T(8,128)S(1)}, u32[]{:S(2)}, u32[]{:S(2)}) collective-permute-start(f32[7,16]{1,0:T(8,128)S(1)} %add.62), channel_id=1, source_target_pairs={{0,64},{32,96},{64,0},{96,32},{128,192},{160,224},{192,128},{224,1... | collective-permute-start | bytes 1352 | tf_op jit(solution)/shard_map/ppermute | solution.py:79
  235.8 1.8 collective-permute-done.4
  237.7 2.9 collective-permute-start.5
  240.6 1.3 collective-permute-start.2
  241.9 0.2 collective-permute-done.5
  242.0 6.3 %collective-permute-start.6 = (f32[7,16]{1,0:T(8,128)S(1)}, f32[7,16]{1,0:T(8,128)S(1)}, u32[]{:S(2)}, u32[]{:S(2)}) collective-permute-start(f32[7,16]{1,0:T(8,128)S(1)} %add.64), channel_id=1, source_target_pairs={{0,256},{32,288},{64,320},{96,352},{128,384},{160,416},{192,448},{... | collective-permute-start | bytes 1352 | tf_op jit(solution)/shard_map/ppermute | solution.py:79
  248.3 41.1 %all-gather.4.cloned.1.call-done = bf16[4096,256]{1,0:T(8,128)(2,1)} async-done(((bf16[256,256]{1,0:T(8,128)(2,1)}), bf16[4096,256]{1,0:T(8,128)(2,1)}) %all-gather.4.cloned.1.call-update) | async-done | bytes 2097168 | tf_op jit(solution)/shard_map/all_gather | solution.py:56
  289.5 4.9 %fusion.20 = f32[256,512]{1,0:T(8,128)} fusion(bf16[4096,256]{1,0:T(8,128)(2,1)} %all-gather.4.cloned.1.call-done, bf16[4096,512]{0,1:T(8,128)(2,1)} %bitcast.34), kind=kOutput, calls=%fused_computation.61 | convolution fusion | flops 1073741824 | bytes 6815744 | tf_op jit(solution)/shard_map/dot_general | solution.py:55
  294.4 0.0 collective-permute-done.6
  294.4 0.6 add.65
  295.0 0.0 collective-permute-done.2
  295.0 0.9 multiply_convert_fusion
  295.9 0.7 multiply_convert_fusion.1
  (20 shorter events, 0.1 us)
Async XLA Ops:
  7.2 126.2 %copy-start = (bf16[256,512]{1,0:T(8,128)(2,1)S(1)}, bf16[256,512]{1,0:T(8,128)(2,1)}, u32[]{:S(2)}) copy-start(bf16[256,512]{1,0:T(8,128)(2,1)} %param.10) | copy-start | bytes 786436
  7.2 112.0 %all-gather.6.cloned.1.call-start = ((), (), s32[]{:S(2)}) async-start(), calls=%async_computation.3 | async-start | bytes 4325376 | tf_op jit(solution)/shard_map/all_gather | solution.py:45
  7.2 1.7 collective-permute-start
  8.9 0.7 copy-start.5
  9.6 215.3 %reduce-scatter.2.cloned.1.call-start = ((), (), s32[]{:S(2)}) async-start(), calls=%async_computation.1 | async-start | bytes 4456448 | tf_op jit(solution)/shard_map/reduce_scatter | solution.py:54
  131.5 1.9 copy-start.1
  136.7 0.9 copy-start.2
  136.7 1.0 copy-start.3
  136.7 4.4 %copy-start.6 = (f32[7,16]{1,0:T(8,128)S(1)}, f32[7,16]{1,0:T(8,128)}, u32[]{:S(2)}) copy-start(f32[7,16]{1,0:T(8,128)} %param.11) | copy-start | bytes 1348
  136.7 5.6 %copy-start.4 = (bf16[256,256]{1,0:T(8,128)(2,1)S(1)}, bf16[256,256]{1,0:T(8,128)(2,1)}, u32[]{:S(2)}) copy-start(bf16[256,256]{1,0:T(8,128)(2,1)} %param.6) | copy-start | bytes 393220
  136.7 152.7 %all-gather.4.cloned.1.call-start = ((), (), s32[]{:S(2)}) async-start(), calls=%async_computation.2 | async-start | bytes 2228224 | tf_op jit(solution)/shard_map/all_gather | solution.py:56
  137.7 4.5 %collective-permute-start.1 = (bf16[2,6,256]{2,1,0:T(8,128)(2,1)S(1)}, bf16[2,6,256]{2,1,0:T(8,128)(2,1)S(1)}, u32[]{:S(2)}, u32[]{:S(2)}) collective-permute-start(bf16[2,6,256]{2,1,0:T(8,128)(2,1)S(1)} %pad_maximum_fusion.1), channel_id=1, source_target_pairs={{0,32},{32,64},{64,96},{96,128},{128,160},{160,192},{192,224},{224... | collective-permute-start | bytes 18440 | tf_op jit(solution)/shard_map/ppermute | solution.py:13
  227.5 4.4 %collective-permute-start.3 = (f32[7,16]{1,0:T(8,128)S(1)}, f32[7,16]{1,0:T(8,128)S(1)}, u32[]{:S(2)}, u32[]{:S(2)}) collective-permute-start(f32[7,16]{1,0:T(8,128)S(1)} %reduce_sum.79), channel_id=1, source_target_pairs={{0,32},{32,0},{64,96},{96,64},{128,160},{160,128},{192,224},{224,1... | collective-permute-start | bytes 1352 | tf_op jit(solution)/shard_map/ppermute | solution.py:79
  231.8 5.8 %collective-permute-start.4 = (f32[7,16]{1,0:T(8,128)S(1)}, f32[7,16]{1,0:T(8,128)S(1)}, u32[]{:S(2)}, u32[]{:S(2)}) collective-permute-start(f32[7,16]{1,0:T(8,128)S(1)} %add.62), channel_id=1, source_target_pairs={{0,64},{32,96},{64,0},{96,32},{128,192},{160,224},{192,128},{224,1... | collective-permute-start | bytes 1352 | tf_op jit(solution)/shard_map/ppermute | solution.py:79
  237.7 4.3 %collective-permute-start.5 = (f32[7,16]{1,0:T(8,128)S(1)}, f32[7,16]{1,0:T(8,128)S(1)}, u32[]{:S(2)}, u32[]{:S(2)}) collective-permute-start(f32[7,16]{1,0:T(8,128)S(1)} %add.63), channel_id=1, source_target_pairs={{0,128},{32,160},{64,192},{96,224},{128,0},{160,32},{192,64},{224,... | collective-permute-start | bytes 1352 | tf_op jit(solution)/shard_map/ppermute | solution.py:79
  240.6 54.4 %collective-permute-start.2 = (f32[6,256]{1,0:T(8,128)S(1)}, f32[6,256]{1,0:T(8,128)S(1)}, u32[]{:S(2)}, u32[]{:S(2)}) collective-permute-start(f32[6,256]{1,0:T(8,128)S(1)} %slice.158), channel_id=1, source_target_pairs={{32,0},{64,32},{96,64},{128,96},{160,128},{192,160},{224,192},{256... | collective-permute-start | bytes 18440 | tf_op jit(solution)/shard_map/ppermute | solution.py:13
  242.0 52.4 %collective-permute-start.6 = (f32[7,16]{1,0:T(8,128)S(1)}, f32[7,16]{1,0:T(8,128)S(1)}, u32[]{:S(2)}, u32[]{:S(2)}) collective-permute-start(f32[7,16]{1,0:T(8,128)S(1)} %add.64), channel_id=1, source_target_pairs={{0,256},{32,288},{64,320},{96,352},{128,384},{160,416},{192,448},{... | collective-permute-start | bytes 1352 | tf_op jit(solution)/shard_map/ppermute | solution.py:79
Sparse Core Ops, SparseCore 0:
  10.7 108.4 all-gather.5
  136.8 88.0 reduce-scatter.1
  228.9 60.4 all-gather.3
